TPU v7x, 256 devices: a whole 4x4x8 slice. The times are simulated.
256 devices in a mesh: outer: 8 (over y_hi, x), inner: 32 (over z, y_lo, core).
Axes of the slice: x: 4, y: 4 (y_hi: 2, y_lo: 2; y = y_hi * 2 + y_lo), z: 8, core: 2. Of those that a mesh axis runs over, the one named last changes fastest.
Arguments:
- weights: float32 [131072, 128], P(('outer', 'inner')), may hold values from -0.375 to 0.375
Outputs:
- level_weights: float32 [131072, 128], P(('outer', 'inner'))
All inputs are finite; a program needn't handle non-finite values.
Results may differ from a plain program's by a relative error of at most 0.0049.
Values sent between devices are 32-bit elements; how exact they have to be, the bound alone decides.
A program may use at most 64 MiB of HBM per device.

v0:
```python
import functools

import jax
import jax.numpy as jnp
import numpy as np
from jax import lax
from jax.experimental import pallas as pl
from jax.experimental.pallas import tpu as pltpu
from jax.sharding import PartitionSpec as P

MESH = pl.DeviceIdType.MESH
F32 = jnp.float32
BF16 = jnp.bfloat16
GRID_N = 16384.0
LEVELS = 8
TILES = 32


def chebyshev_nodes():
    return 0.5 * np.cos(np.pi * (2.0 * np.arange(8) + 1.0) / 16.0)


def lagrange_weights(which_child):
    node = chebyshev_nodes()
    targets = (node + which_child - 0.5) / 2.0
    table = np.ones((8, 8))
    for anchor in range(8):
        for other in range(8):
            if other != anchor:
                table[anchor] *= (targets - node[other]) / (node[anchor] - node[other])
    return table


def merge_matrix(dimension):
    parts = []
    for child in range(2):
        table = lagrange_weights(child)
        full = np.kron(table, np.eye(8)) if dimension == 0 else np.kron(np.eye(8), table)
        parts.append(full.T)
    one = np.concatenate(parts, axis=0)
    out = np.zeros((256, 128))
    out[:128, :64] = one
    out[128:, 64:] = one
    return out


def even_fit(values, terms):
    z = 0.125 * (1.0 - np.cos(np.pi * (np.arange(400) + 0.5) / 400))
    basis = np.polynomial.chebyshev.Chebyshev.fit(z, values(np.sqrt(z)), terms - 1, domain=[0, 0.25])
    return [float(c) for c in basis.convert(kind=np.polynomial.Polynomial).coef]


SIN_COEF = even_fit(lambda f: np.sin(2 * np.pi * f) / f, 6)
COS_COEF = even_fit(lambda f: np.cos(2 * np.pi * f), 7)


def horner(coef, z):
    total = jnp.full_like(z, coef[-1])
    for c in coef[-2::-1]:
        total = total * z + c
    return total


def nearest(v):
    return jnp.floor(v + 0.5)


def turn(cycles):
    f = cycles - nearest(cycles)
    z = f * f
    return horner(COS_COEF, z), f * horner(SIN_COEF, z)


def widths(level):
    odd = len([m for m in range(level) if m % 2 == 1])
    even = len([m for m in range(level) if m % 2 == 0])
    h = (2.0 ** -(3 + 4 - odd), 2.0 ** -(4 + 4 - even))
    w = (GRID_N * 2.0 ** -(4 + odd), GRID_N * 2.0 ** -(3 + even))
    return h, w


def place_terms(level):
    terms = []
    for m in range(level, LEVELS):
        e = (m + 1) % 2
        weight = 2.0 ** -(7 - (m - 1) // 2) if e == 0 else 2.0 ** -(8 - m // 2)
        if m == level:
            where = ("lane", 6)
        elif m <= 5:
            where = ("lead", m - 1)
        else:
            where = ("sub", m - 5)
        terms.append((*where, e, weight))
    return terms


def frequency_terms(level):
    terms = [("sub", 0, 0, 1024.0)]
    for m in range(level):
        e = (m + 1) % 2
        weight = 512.0 / 2 ** (m // 2) if e == 0 else 1024.0 / 2 ** (m // 2)
        if m <= 4:
            where = ("lead", m)
        elif m <= 6:
            where = ("sub", m - 4)
        else:
            where = ("lane", 6)
        terms.append((*where, e, weight))
    return terms


def vector_part(terms, e, sub, lane, base):
    total = jnp.full((8, 128), base, F32)
    for where, bit, dim, weight in terms:
        if dim == e and where != "lead":
            source = sub if where == "sub" else lane
            total = total + ((source >> bit) & 1).astype(F32) * weight
    return total


def lead_part(terms, e, index, scale):
    total = jnp.int32(0)
    for where, bit, dim, weight in terms:
        if dim == e and where == "lead":
            total = total + ((index >> bit) & 1) * int(weight * scale)
    return total


def grid_offset(level):
    return sum(max(TILES >> l, 1) for l in range(level))


GRID_TILES = grid_offset(LEVELS + 1)


def device_bits(dest):
    d1 = ((dest >> 6) & 1) + 2 * ((dest >> 7) & 1) + 4 * (dest & 1)
    d2 = (dest >> 1) & 15
    d5 = (dest >> 5) & 1
    return d1, d2, d5


def coefficient_tiles(me, tau_ref, g_ref, sub, lane):
    d1, d2, _ = device_bits(me)
    tau = (tau_ref[0:1, :], tau_ref[1:2, :])
    for level in range(LEVELS + 1):
        h, _ = widths(level)
        terms = place_terms(level)
        base = [vector_part(terms, e, sub, lane, 0.5 * h[e]) + h[e] * tau[e] for e in range(2)]
        count = max(TILES >> level, 1)

        def tile(u, carry, level=level, base=base, terms=terms):
            index = u << level
            x1 = base[0] + (d1 * 32 + lead_part(terms, 0, index, 256)).astype(F32) * (1 / 256)
            x2 = base[1] + (d2 * 16 + lead_part(terms, 1, index, 256)).astype(F32) * (1 / 256)
            cos1, sin1 = turn(x1)
            cos2, sin2 = turn(x2)
            g1 = (2.0 + sin1 * sin2) * (1 / 16)
            g2 = (2.0 + cos1 * cos2) * (1 / 16)
            g_ref[0, grid_offset(level) + u] = g1 * g1
            g_ref[1, grid_offset(level) + u] = g2 * g2
            return carry

        lax.fori_loop(0, count, tile, 0, unroll=min(count, 2))


def factor_tiles(me, level, tau_ref, g_ref, cos_ref, sin_ref, sub, lane):
    _, _, d5 = device_bits(me)
    tau = (tau_ref[0:1, :], tau_ref[1:2, :])
    h, w = widths(level)
    e = (level + 1) % 2
    terms = frequency_terms(level)
    base = [vector_part(terms, d, sub, lane, 0.5 * w[d] - GRID_N / 2) for d in range(2)]
    slope = [h[d] * tau[d] for d in range(2)]

    def whole(k1, k2, g1, g2):
        lin = slope[0] * k1 + slope[1] * k2
        rad = jnp.sqrt(g1 * (k1 * k1) + g2 * (k2 * k2))
        return (lin - nearest(lin)) + (rad - nearest(rad))

    def tile(i, carry):
        k1 = base[0] + lead_part(terms, 0, i, 1).astype(F32)
        k2 = base[1] + (d5 * 2048 + lead_part(terms, 1, i, 1)).astype(F32)
        u = grid_offset(level) + (i >> min(level, 5))
        g1, g2 = g_ref[0, u], g_ref[1, u]
        if level == LEVELS:
            cos_ref[2 * level, i], sin_ref[2 * level, i] = turn(whole(k1, k2, g1, g2))
            return carry
        if level > 0:
            square = g1 * (k1 * k1) + g2 * (k2 * k2)
            rad = jnp.sqrt(square)
        for j in range(2):
            step = (2 * j - 1) * w[e] / 4
            if level == 0:
                cycles = whole(k1, k2 + step, g1, g2)
            else:
                k, g = (k1, g1) if e == 0 else (k2, g2)
                extra = g * (step * (2.0 * k + step))
                cycles = slope[e] * step + extra / (jnp.sqrt(square + extra) + rad)
            cos_ref[2 * level + j, i], sin_ref[2 * level + j, i] = turn(cycles)
        return carry

    lax.fori_loop(0, TILES, tile, 0, unroll=2)


def split(value):
    high = value.astype(BF16)
    low = (value - high.astype(F32)).astype(BF16)
    return high, low


def merge(left, right, w_high, w_low):
    n = left.shape[0]
    lh, ll = split(left)
    rh, rl = split(right)
    high = jnp.concatenate([lh.reshape(8 * n, 128), rh.reshape(8 * n, 128)], axis=1)
    low = jnp.concatenate([ll.reshape(8 * n, 128), rl.reshape(8 * n, 128)], axis=1)
    total = jnp.dot(high, w_high, preferred_element_type=F32)
    total += jnp.dot(low, w_high, preferred_element_type=F32)
    total += jnp.dot(high, w_low, preferred_element_type=F32)
    return total.reshape(n, 8, 128)


def run_levels(recv, out_ref, cos_ref, sin_ref, w_refs, state, sub, lane):
    low_lane = lane < 64
    first, second = recv[0], recv[1]
    first_t, second_t = pltpu.roll(first, 64, 2), pltpu.roll(second, 64, 2)
    state[0] = jnp.where(low_lane[None], first, second_t)
    state[1] = jnp.where(low_lane[None], first_t, second)
    for level in range(LEVELS):
        e = (level + 1) % 2
        w_high, w_low = w_refs[2 * e][...], w_refs[2 * e + 1][...]
        re, im = state[0], state[1]
        turned = []
        for j in range(2):
            c, s = cos_ref[2 * level + j], sin_ref[2 * level + j]
            turned.append((re * c - im * s, im * c + re * s))
        for part in range(2):
            r0, r1 = turned[0][part], turned[1][part]
            if level < 5:
                lo = 1 << level
                hi = TILES // (2 * lo)
                outs = []
                for r in (r0, r1):
                    v = r.reshape(hi, 2, lo, 8, 128)
                    left = v[:, 0].reshape(16, 8, 128)
                    right = v[:, 1].reshape(16, 8, 128)
                    outs.append(merge(left, right, w_high, w_low).reshape(hi, 1, lo, 8, 128))
                new = jnp.concatenate(outs, axis=1).reshape(TILES, 8, 128)
            elif level < 7:
                bit = level - 4
                keep = (((sub >> bit) & 1) == 0)[None]
                shift = 1 << bit
                left = jnp.where(keep, r0, pltpu.roll(r1, shift, 1))
                right = jnp.where(keep, pltpu.roll(r0, 8 - shift, 1), r1)
                new = merge(left, right, w_high, w_low)
            else:
                new = merge(r0, r1, w_high, w_low)
            state[part] = new
    re, im = state[0], state[1]
    c, s = cos_ref[2 * LEVELS], sin_ref[2 * LEVELS]
    w_re, w_im = re * c + im * s, im * c - re * s
    even = jnp.where(low_lane[None], w_re, pltpu.roll(w_im, 64, 2))
    odd = jnp.where(low_lane[None], pltpu.roll(w_re, 64, 2), w_im)
    out_ref[...] = jnp.concatenate([even[:, None], odd[:, None]], axis=1)


def mesh_id(d):
    return (d >> 5, d & 31)


def kernel(x_ref, tau_ref, w0, w1, w2, w3, out_ref, recv, state, g_ref, cos_ref, sin_ref, send_sem, recv_sem, own_sem):
    me = lax.axis_index("outer") * 32 + lax.axis_index("inner")
    barrier = pltpu.get_barrier_semaphore()

    def greet(k, carry):
        pl.semaphore_signal(barrier, inc=1, device_id=mesh_id((me + k) & 255), device_id_type=MESH)
        return carry

    lax.fori_loop(1, 256, greet, 0, unroll=5)
    sub = lax.broadcasted_iota(jnp.int32, (8, 128), 0)
    lane = lax.broadcasted_iota(jnp.int32, (8, 128), 1)
    coefficient_tiles(me, tau_ref, g_ref, sub, lane)
    for level in range(LEVELS + 1):
        factor_tiles(me, level, tau_ref, g_ref, cos_ref, sin_ref, sub, lane)
    pl.semaphore_wait(barrier, 255)
    place = recv.at[me & 1, (me >> 1) & 31, me >> 6]
    own = pltpu.make_async_copy(x_ref.at[(me & 31) * 8 + (me >> 5)], place, own_sem)
    own.start()

    def send(k, carry):
        d = (me + k) & 255
        pltpu.make_async_remote_copy(
            src_ref=x_ref.at[(d & 31) * 8 + (d >> 5)],
            dst_ref=place,
            send_sem=send_sem,
            recv_sem=recv_sem,
            device_id=mesh_id(d),
            device_id_type=MESH,
        ).start()
        return carry

    lax.fori_loop(1, 256, send, 0, unroll=5)
    own.wait()
    most = x_ref.at[pl.ds(0, 255)]
    pltpu.make_async_copy(most, most, recv_sem).wait()
    pltpu.make_async_copy(most, most, send_sem).wait()
    run_levels(recv.reshape(2, TILES, 8, 128), out_ref, cos_ref, sin_ref, (w0, w1, w2, w3), state, sub, lane)


def body(weights):
    tables = []
    for dimension in range(2):
        full = jnp.asarray(merge_matrix(dimension), F32)
        high = full.astype(BF16)
        tables += [high, (full - high.astype(F32)).astype(BF16)]
    lanes = np.arange(128)
    node = chebyshev_nodes()
    tau = np.zeros((8, 128))
    tau[0], tau[1] = node[(lanes >> 3) & 7], node[lanes & 7]
    vmem = pl.BlockSpec(memory_space=pltpu.VMEM)
    out = pl.pallas_call(
        kernel,
        out_shape=jax.ShapeDtypeStruct((TILES, 2, 8, 128), F32),
        in_specs=[pl.BlockSpec(memory_space=pltpu.HBM)] + [vmem] * 5,
        out_specs=vmem,
        scratch_shapes=[
            pltpu.VMEM((2, TILES, 4, 2, 128), F32),
            pltpu.VMEM((2, TILES, 8, 128), F32),
            pltpu.VMEM((2, GRID_TILES, 8, 128), F32),
            pltpu.VMEM((2 * LEVELS + 1, TILES, 8, 128), F32),
            pltpu.VMEM((2 * LEVELS + 1, TILES, 8, 128), F32),
            pltpu.SemaphoreType.DMA,
            pltpu.SemaphoreType.DMA,
            pltpu.SemaphoreType.DMA,
        ],
        compiler_params=pltpu.CompilerParams(collective_id=0, has_side_effects=True),
    )(weights.reshape(256, 2, 128), jnp.asarray(tau, F32), *tables)
    return out.reshape(512, 128)


def solution(mesh):
    spec = P(("outer", "inner"), None)
    return jax.shard_map(body, mesh=mesh, in_specs=(spec,), out_specs=spec, check_vma=False)
```

profile of v0, /device:TPU:1, one launch (start us, length us, event | category | flops | bytes accessed | tf_op | source)
XLA Modules:
  0.0 34.6 jit_solution(8460065547451103772)
XLA Ops:
  0.0 32.9 %shard_map.46 = f32[32,2,8,128]{3,2,1,0:T(8,128)} custom-call(f32[256,2,128]{2,1,0:T(2,128)} %bitcast.3, f32[8,128]{1,0:T(8,128)} %constant.8.clone.tau_ref, bf16[256,128]{1,0:T(8,128)(2,1)} %constant.9.w0, bf16[256,128]{1,0:T(8,128)(2,1)} %constant.12.w1, bf16[256,128]{1,0:T(8,128)(2,1)} %constant.13.w2, bf16[256,128]{1,0:T(8,128)(2,1)} %constant.16.w3), custom_call_target="tpu_custom_call" | custom-call | tf_op jit(solution)/shard_map/pallas_call | solution.py:322
  32.9 1.7 %copy.6 = f32[512,128]{1,0:T(8,128)} copy(f32[512,128]{1,0:T(8,128)} %bitcast.2) | data formatting | bytes 524288
where the time goes:
time: 34.7 us; the launch traced here: 34.6 us
  Pallas kernels  32.9 us (95%)
  local copies, waits for them, and re-layouts  1.67 us (5%)
    pallas_call x1, Pallas kernels, body(): pl.pallas_call(kernel, out_shape=jax.ShapeDtypeStruct((TILES, 2, 8, 128),...  32.9 us
    unnamed x1, local copies, waits for them, and re-layouts  1.67 us

commit v1 on v0

--- a/solution.py
+++ b/solution.py
@@ -8,7 +8,7 @@
 from jax.experimental.pallas import tpu as pltpu
 from jax.sharding import PartitionSpec as P
 
-MESH = pl.DeviceIdType.MESH
+LOGICAL = pl.DeviceIdType.LOGICAL
 F32 = jnp.float32
 BF16 = jnp.bfloat16
 GRID_N = 16384.0
@@ -221,7 +221,7 @@
     return total.reshape(n, 8, 128)
 
 
-def run_levels(recv, out_ref, cos_ref, sin_ref, w_refs, state, sub, lane):
+def run_levels(recv, out_ref, cos_ref, sin_ref, w_ref, state, sub, lane):
     low_lane = lane < 64
     first, second = recv[0], recv[1]
     first_t, second_t = pltpu.roll(first, 64, 2), pltpu.roll(second, 64, 2)
@@ -229,7 +229,7 @@
     state[1] = jnp.where(low_lane[None], first_t, second)
     for level in range(LEVELS):
         e = (level + 1) % 2
-        w_high, w_low = w_refs[2 * e][...], w_refs[2 * e + 1][...]
+        w_high, w_low = w_ref[2 * e], w_ref[2 * e + 1]
         re, im = state[0], state[1]
         turned = []
         for j in range(2):
@@ -265,47 +265,59 @@
     out_ref[...] = jnp.concatenate([even[:, None], odd[:, None]], axis=1)
 
 
-def mesh_id(d):
-    return (d >> 5, d & 31)
-
-
-def kernel(x_ref, tau_ref, w0, w1, w2, w3, out_ref, recv, state, g_ref, cos_ref, sin_ref, send_sem, recv_sem, own_sem):
+FAR = 0xD0
+
+
+def farthest_first(n):
+    return n ^ FAR
+
+
+def over_others(action):
+    def step(n, carry):
+        action(farthest_first(n))
+        return carry
+
+    lax.fori_loop(0, FAR, step, 0, unroll=8)
+    lax.fori_loop(FAR + 1, 256, step, 0, unroll=47)
+
+
+def kernel(x_ref, tau_hbm, w_hbm, out_ref, recv, state, g_ref, cos_ref, sin_ref, tau_ref, w_ref, send_sem, recv_sem, own_sem, table_sem):
     me = lax.axis_index("outer") * 32 + lax.axis_index("inner")
     barrier = pltpu.get_barrier_semaphore()
-
-    def greet(k, carry):
-        pl.semaphore_signal(barrier, inc=1, device_id=mesh_id((me + k) & 255), device_id_type=MESH)
-        return carry
-
-    lax.fori_loop(1, 256, greet, 0, unroll=5)
+    over_others(lambda k: pl.semaphore_signal(barrier, inc=1, device_id=me ^ k, device_id_type=LOGICAL))
+    place = recv.at[me & 1, (me >> 1) & 31, me >> 6]
+    copies = [
+        pltpu.make_async_copy(tau_hbm, tau_ref, table_sem.at[0]),
+        pltpu.make_async_copy(w_hbm, w_ref, table_sem.at[1]),
+        pltpu.make_async_copy(x_ref.at[(me & 31) * 8 + (me >> 5)], place, own_sem),
+    ]
+    for copy in copies:
+        copy.start()
     sub = lax.broadcasted_iota(jnp.int32, (8, 128), 0)
     lane = lax.broadcasted_iota(jnp.int32, (8, 128), 1)
-    coefficient_tiles(me, tau_ref, g_ref, sub, lane)
-    for level in range(LEVELS + 1):
-        factor_tiles(me, level, tau_ref, g_ref, cos_ref, sin_ref, sub, lane)
     pl.semaphore_wait(barrier, 255)
-    place = recv.at[me & 1, (me >> 1) & 31, me >> 6]
-    own = pltpu.make_async_copy(x_ref.at[(me & 31) * 8 + (me >> 5)], place, own_sem)
-    own.start()
-
-    def send(k, carry):
-        d = (me + k) & 255
+
+    def send(k):
+        d = me ^ k
         pltpu.make_async_remote_copy(
             src_ref=x_ref.at[(d & 31) * 8 + (d >> 5)],
             dst_ref=place,
             send_sem=send_sem,
             recv_sem=recv_sem,
-            device_id=mesh_id(d),
-            device_id_type=MESH,
+            device_id=d,
+            device_id_type=LOGICAL,
         ).start()
-        return carry
-
-    lax.fori_loop(1, 256, send, 0, unroll=5)
-    own.wait()
+
+    over_others(send)
+    for copy in copies:
+        copy.wait()
+    coefficient_tiles(me, tau_ref, g_ref, sub, lane)
+    for level in range(LEVELS + 1):
+        factor_tiles(me, level, tau_ref, g_ref, cos_ref, sin_ref, sub, lane)
     most = x_ref.at[pl.ds(0, 255)]
     pltpu.make_async_copy(most, most, recv_sem).wait()
     pltpu.make_async_copy(most, most, send_sem).wait()
-    run_levels(recv.reshape(2, TILES, 8, 128), out_ref, cos_ref, sin_ref, (w0, w1, w2, w3), state, sub, lane)
+    run_levels(recv.reshape(2, TILES, 8, 128), out_ref, cos_ref, sin_ref, w_ref, state, sub, lane)
 
 
 def body(weights):
@@ -321,8 +333,8 @@
     vmem = pl.BlockSpec(memory_space=pltpu.VMEM)
     out = pl.pallas_call(
         kernel,
-        out_shape=jax.ShapeDtypeStruct((TILES, 2, 8, 128), F32),
-        in_specs=[pl.BlockSpec(memory_space=pltpu.HBM)] + [vmem] * 5,
+        out_shape=pltpu.VMEM((TILES, 2, 8, 128), F32),
+        in_specs=[pl.BlockSpec(memory_space=pltpu.HBM)] * 3,
         out_specs=vmem,
         scratch_shapes=[
             pltpu.VMEM((2, TILES, 4, 2, 128), F32),
@@ -330,12 +342,15 @@
             pltpu.VMEM((2, GRID_TILES, 8, 128), F32),
             pltpu.VMEM((2 * LEVELS + 1, TILES, 8, 128), F32),
             pltpu.VMEM((2 * LEVELS + 1, TILES, 8, 128), F32),
+            pltpu.VMEM((8, 128), F32),
+            pltpu.VMEM((4, 256, 128), BF16),
             pltpu.SemaphoreType.DMA,
             pltpu.SemaphoreType.DMA,
             pltpu.SemaphoreType.DMA,
+            pltpu.SemaphoreType.DMA((2,)),
         ],
         compiler_params=pltpu.CompilerParams(collective_id=0, has_side_effects=True),
-    )(weights.reshape(256, 2, 128), jnp.asarray(tau, F32), *tables)
+    )(weights.reshape(256, 2, 128), jnp.asarray(tau, F32), jnp.stack(tables))
     return out.reshape(512, 128)
 
 

time: 34.7 us -> 27.1 us (0.78)
  Pallas kernels: 32.9 us -> 26.3 us
  local copies, waits for them, and re-layouts: 1.67 us -> 0.71 us
    pallas_call x1, Pallas kernels: 32.9 us -> 26.3 us  [body(): pl.pallas_call(kernel, out_shape=pltpu.VMEM((TILES, 2, 8, 128), F32), in_...]
    unnamed x1, local copies, waits for them, and re-layouts: 1.67 us -> 0.71 us
where the time goes in v1:
time: 27.1 us; the launch traced here: 27 us
  Pallas kernels  26.3 us (97%)
  local copies, waits for them, and re-layouts  0.71 us (3%)
    pallas_call x1, Pallas kernels, body(): pl.pallas_call(kernel, out_shape=pltpu.VMEM((TILES, 2, 8, 128), F32), in_...  26.3 us
    unnamed x1, local copies, waits for them, and re-layouts  0.71 us

profile of v1, /device:TPU:1, one launch (start us, length us, event | category | flops | bytes accessed | tf_op | source)
XLA Modules:
  0.0 27.0 jit_solution(12107086470284745505)
XLA Ops:
  0.0 26.3 %shard_map.46 = f32[32,2,8,128]{3,2,1,0:T(8,128)S(1)} custom-call(f32[256,2,128]{2,1,0:T(2,128)} %bitcast.3, f32[8,128]{1,0:T(8,128)} %constant.8.clone.tau_hbm, bf16[4,256,128]{2,1,0:T(8,128)(2,1)} %constant.21.w_hbm), custom_call_target="tpu_custom_call" | custom-call | tf_op jit(solution)/shard_map/pallas_call | solution.py:334
  26.3 0.7 %copy.6 = f32[512,128]{1,0:T(8,128)} copy(f32[512,128]{1,0:T(8,128)S(1)} %bitcast.2) | data formatting | bytes 524288

commit v2 on v1

--- a/solution.py
+++ b/solution.py
@@ -14,6 +14,8 @@
 GRID_N = 16384.0
 LEVELS = 8
 TILES = 32
+EARLY_PLANES = 2
+EXACT = (0, 1, 2, 3, 4, 5, 6, 7)
 
 
 def chebyshev_nodes():
@@ -161,7 +163,7 @@
             g_ref[1, grid_offset(level) + u] = g2 * g2
             return carry
 
-        lax.fori_loop(0, count, tile, 0, unroll=min(count, 2))
+        lax.fori_loop(0, count, tile, 0, unroll=min(count, 8))
 
 
 def factor_tiles(me, level, tau_ref, g_ref, cos_ref, sin_ref, sub, lane):
@@ -200,36 +202,32 @@
             cos_ref[2 * level + j, i], sin_ref[2 * level + j, i] = turn(cycles)
         return carry
 
-    lax.fori_loop(0, TILES, tile, 0, unroll=2)
-
-
-def split(value):
-    high = value.astype(BF16)
-    low = (value - high.astype(F32)).astype(BF16)
-    return high, low
-
-
-def merge(left, right, w_high, w_low):
+    lax.fori_loop(0, TILES, tile, 0, unroll=8)
+
+
+def merge(left, right, w_ref, dimension, exact):
     n = left.shape[0]
-    lh, ll = split(left)
-    rh, rl = split(right)
-    high = jnp.concatenate([lh.reshape(8 * n, 128), rh.reshape(8 * n, 128)], axis=1)
-    low = jnp.concatenate([ll.reshape(8 * n, 128), rl.reshape(8 * n, 128)], axis=1)
-    total = jnp.dot(high, w_high, preferred_element_type=F32)
-    total += jnp.dot(low, w_high, preferred_element_type=F32)
-    total += jnp.dot(high, w_low, preferred_element_type=F32)
-    return total.reshape(n, 8, 128)
-
-
-def run_levels(recv, out_ref, cos_ref, sin_ref, w_ref, state, sub, lane):
+    values = [left.reshape(8 * n, 128), right.reshape(8 * n, 128)]
+    parts = [v.astype(BF16) for v in values]
+    if exact:
+        parts += [(v - p.astype(F32)).astype(BF16) for v, p in zip(values, parts)]
+    table = w_ref[dimension, : 128 * len(parts)]
+    total = jnp.dot(jnp.concatenate(parts, axis=1), table, preferred_element_type=F32)
+    return (total[:, :128] + total[:, 128:]).reshape(n, 8, 128)
+
+
+def load(recv, state, lane):
+    low_lane = (lane < 64)[None]
+    first, second = recv[0], recv[1]
+    state[0] = jnp.where(low_lane, first, pltpu.roll(second, 64, 2))
+    state[1] = jnp.where(low_lane, pltpu.roll(first, 64, 2), second)
+
+
+def run_levels(out_ref, cos_ref, sin_ref, w_ref, state, sub, lane):
     low_lane = lane < 64
-    first, second = recv[0], recv[1]
-    first_t, second_t = pltpu.roll(first, 64, 2), pltpu.roll(second, 64, 2)
-    state[0] = jnp.where(low_lane[None], first, second_t)
-    state[1] = jnp.where(low_lane[None], first_t, second)
     for level in range(LEVELS):
         e = (level + 1) % 2
-        w_high, w_low = w_ref[2 * e], w_ref[2 * e + 1]
+        exact = level in EXACT
         re, im = state[0], state[1]
         turned = []
         for j in range(2):
@@ -245,7 +243,7 @@
                     v = r.reshape(hi, 2, lo, 8, 128)
                     left = v[:, 0].reshape(16, 8, 128)
                     right = v[:, 1].reshape(16, 8, 128)
-                    outs.append(merge(left, right, w_high, w_low).reshape(hi, 1, lo, 8, 128))
+                    outs.append(merge(left, right, w_ref, e, exact).reshape(hi, 1, lo, 8, 128))
                 new = jnp.concatenate(outs, axis=1).reshape(TILES, 8, 128)
             elif level < 7:
                 bit = level - 4
@@ -253,9 +251,9 @@
                 shift = 1 << bit
                 left = jnp.where(keep, r0, pltpu.roll(r1, shift, 1))
                 right = jnp.where(keep, pltpu.roll(r0, 8 - shift, 1), r1)
-                new = merge(left, right, w_high, w_low)
+                new = merge(left, right, w_ref, e, exact)
             else:
-                new = merge(r0, r1, w_high, w_low)
+                new = merge(r0, r1, w_ref, e, exact)
             state[part] = new
     re, im = state[0], state[1]
     c, s = cos_ref[2 * LEVELS], sin_ref[2 * LEVELS]
@@ -295,6 +293,18 @@
         copy.start()
     sub = lax.broadcasted_iota(jnp.int32, (8, 128), 0)
     lane = lax.broadcasted_iota(jnp.int32, (8, 128), 1)
+    copies[0].wait()
+    early = ((me >> 2) & 7) < EARLY_PLANES
+
+    def factors():
+        coefficient_tiles(me, tau_ref, g_ref, sub, lane)
+        for level in range(LEVELS + 1):
+            factor_tiles(me, level, tau_ref, g_ref, cos_ref, sin_ref, sub, lane)
+
+    @pl.when(early)
+    def _():
+        factors()
+
     pl.semaphore_wait(barrier, 255)
 
     def send(k):
@@ -309,15 +319,19 @@
         ).start()
 
     over_others(send)
-    for copy in copies:
+    for copy in copies[1:]:
         copy.wait()
-    coefficient_tiles(me, tau_ref, g_ref, sub, lane)
-    for level in range(LEVELS + 1):
-        factor_tiles(me, level, tau_ref, g_ref, cos_ref, sin_ref, sub, lane)
+
+    @pl.when(jnp.logical_not(early))
+    def _():
+        factors()
+
     most = x_ref.at[pl.ds(0, 255)]
+
     pltpu.make_async_copy(most, most, recv_sem).wait()
+    load(recv.reshape(2, TILES, 8, 128), state, lane)
+    run_levels(out_ref, cos_ref, sin_ref, w_ref, state, sub, lane)
     pltpu.make_async_copy(most, most, send_sem).wait()
-    run_levels(recv.reshape(2, TILES, 8, 128), out_ref, cos_ref, sin_ref, w_ref, state, sub, lane)
 
 
 def body(weights):
@@ -325,7 +339,8 @@
     for dimension in range(2):
         full = jnp.asarray(merge_matrix(dimension), F32)
         high = full.astype(BF16)
-        tables += [high, (full - high.astype(F32)).astype(BF16)]
+        low = (full - high.astype(F32)).astype(BF16)
+        tables.append(jnp.block([[high, low], [high, jnp.zeros_like(low)]]))
     lanes = np.arange(128)
     node = chebyshev_nodes()
     tau = np.zeros((8, 128))
@@ -343,7 +358,7 @@
             pltpu.VMEM((2 * LEVELS + 1, TILES, 8, 128), F32),
             pltpu.VMEM((2 * LEVELS + 1, TILES, 8, 128), F32),
             pltpu.VMEM((8, 128), F32),
-            pltpu.VMEM((4, 256, 128), BF16),
+            pltpu.VMEM((2, 512, 256), BF16),
             pltpu.SemaphoreType.DMA,
             pltpu.SemaphoreType.DMA,
             pltpu.SemaphoreType.DMA,

time: 27.1 us -> 25.2 us (0.930)
  Pallas kernels: 26.3 us -> 24.4 us
    pallas_call x1, Pallas kernels: 26.3 us -> 24.4 us  [body(): pl.pallas_call(kernel, out_shape=pltpu.VMEM((TILES, 2, 8, 128), F32), in_...]
where the time goes in v2:
time: 25.2 us; the launch traced here: 25.1 us
  Pallas kernels  24.4 us (97%)
  local copies, waits for them, and re-layouts  0.71 us (3%)
    pallas_call x1, Pallas kernels, body(): pl.pallas_call(kernel, out_shape=pltpu.VMEM((TILES, 2, 8, 128), F32), in_...  24.4 us
    unnamed x1, local copies, waits for them, and re-layouts  0.71 us

profile of v2, /device:TPU:1, one launch (start us, length us, event | category | flops | bytes accessed | tf_op | source)
XLA Modules:
  0.0 25.1 jit_solution(12690095897651589054)
XLA Ops:
  0.0 24.4 %shard_map.46 = f32[32,2,8,128]{3,2,1,0:T(8,128)S(1)} custom-call(f32[256,2,128]{2,1,0:T(2,128)} %bitcast.3, f32[8,128]{1,0:T(8,128)} %constant.10.clone.tau_hbm, bf16[2,512,256]{2,1,0:T(8,128)(2,1)} %constant.31.w_hbm), custom_call_target="tpu_custom_call" | custom-call | tf_op jit(solution)/shard_map/pallas_call | solution.py:349
  24.4 0.7 %copy.6 = f32[512,128]{1,0:T(8,128)} copy(f32[512,128]{1,0:T(8,128)S(1)} %bitcast.2) | data formatting | bytes 524288

commit v3 on v2

--- a/solution.py
+++ b/solution.py
@@ -266,23 +266,17 @@
 FAR = 0xD0
 
 
-def farthest_first(n):
-    return n ^ FAR
-
-
-def over_others(action):
-    def step(n, carry):
-        action(farthest_first(n))
-        return carry
-
-    lax.fori_loop(0, FAR, step, 0, unroll=8)
-    lax.fori_loop(FAR + 1, 256, step, 0, unroll=47)
-
-
-def kernel(x_ref, tau_hbm, w_hbm, out_ref, recv, state, g_ref, cos_ref, sin_ref, tau_ref, w_ref, send_sem, recv_sem, own_sem, table_sem):
+def kernel(x_ref, tau_hbm, w_hbm, out_ref, recv, state, g_ref, cos_ref, sin_ref, tau_ref, w_ref, send_sem, recv_sem, own_sem, table_sem, ready_sem):
     me = lax.axis_index("outer") * 32 + lax.axis_index("inner")
     barrier = pltpu.get_barrier_semaphore()
-    over_others(lambda k: pl.semaphore_signal(barrier, inc=1, device_id=me ^ k, device_id_type=LOGICAL))
+
+    def greet(n, carry):
+        pl.semaphore_signal(barrier, inc=1, device_id=me ^ (2 * n ^ FAR), device_id_type=LOGICAL)
+        return carry
+
+    lax.fori_loop(0, FAR // 2, greet, 0, unroll=8)
+    lax.fori_loop(FAR // 2 + 1, 128, greet, 0, unroll=23)
+    pl.semaphore_signal(barrier, inc=1, device_id=me ^ 1, device_id_type=LOGICAL)
     place = recv.at[me & 1, (me >> 1) & 31, me >> 6]
     copies = [
         pltpu.make_async_copy(tau_hbm, tau_ref, table_sem.at[0]),
@@ -305,10 +299,10 @@
     def _():
         factors()
 
-    pl.semaphore_wait(barrier, 255)
-
-    def send(k):
-        d = me ^ k
+    pl.semaphore_wait(barrier, 128)
+    pl.semaphore_signal(ready_sem, inc=1, device_id=me ^ 1, device_id_type=LOGICAL)
+
+    def send(d):
         pltpu.make_async_remote_copy(
             src_ref=x_ref.at[(d & 31) * 8 + (d >> 5)],
             dst_ref=place,
@@ -318,7 +312,34 @@
             device_id_type=LOGICAL,
         ).start()
 
-    over_others(send)
+    def serve(other):
+        base = me ^ FAR ^ other
+
+        def step(n, carry):
+            send(base ^ (2 * n))
+            return carry
+
+        lax.fori_loop(0, FAR // 2, step, 0, unroll=8)
+
+        @pl.when(other == 1)
+        def _():
+            send(base ^ FAR)
+
+        lax.fori_loop(FAR // 2 + 1, 128, step, 0, unroll=23)
+
+    core = me & 1
+
+    @pl.when(core == 0)
+    def _():
+        pl.semaphore_wait(ready_sem, 1)
+
+    serve(1 - core)
+
+    @pl.when(core == 1)
+    def _():
+        pl.semaphore_wait(ready_sem, 1)
+
+    serve(core)
     for copy in copies[1:]:
         copy.wait()
 
@@ -363,6 +384,7 @@
             pltpu.SemaphoreType.DMA,
             pltpu.SemaphoreType.DMA,
             pltpu.SemaphoreType.DMA((2,)),
+            pltpu.SemaphoreType.REGULAR,
         ],
         compiler_params=pltpu.CompilerParams(collective_id=0, has_side_effects=True),
     )(weights.reshape(256, 2, 128), jnp.asarray(tau, F32), jnp.stack(tables))

time: 25.2 us -> 24 us (0.952)
  the two profiles are of different devices: /device:TPU:1 before, /device:TPU:2 now
where the time goes in v3:
time: 24 us; the launch traced here: 23.9 us
  Pallas kernels  23.2 us (97%)
  local copies, waits for them, and re-layouts  0.71 us (3%)
    pallas_call x1, Pallas kernels, body(): pl.pallas_call(kernel, out_shape=pltpu.VMEM((TILES, 2, 8, 128), F32), in_...  23.2 us
    unnamed x1, local copies, waits for them, and re-layouts  0.71 us

profile of v3, /device:TPU:2, one launch (start us, length us, event | category | flops | bytes accessed | tf_op | source)
XLA Modules:
  0.0 23.9 jit_solution(11894008326769465013)
XLA Ops:
  0.0 23.2 %shard_map.46 = f32[32,2,8,128]{3,2,1,0:T(8,128)S(1)} custom-call(f32[256,2,128]{2,1,0:T(2,128)} %bitcast.3, f32[8,128]{1,0:T(8,128)} %constant.10.clone.tau_hbm, bf16[2,512,256]{2,1,0:T(8,128)(2,1)} %constant.31.w_hbm), custom_call_target="tpu_custom_call" | custom-call | tf_op jit(solution)/shard_map/pallas_call | solution.py:370
  23.2 0.7 %copy.6 = f32[512,128]{1,0:T(8,128)} copy(f32[512,128]{1,0:T(8,128)S(1)} %bitcast.2) | data formatting | bytes 524288

commit v4 on v3

--- a/solution.py
+++ b/solution.py
@@ -205,15 +205,50 @@
     lax.fori_loop(0, TILES, tile, 0, unroll=8)
 
 
-def merge(left, right, w_ref, dimension, exact):
-    n = left.shape[0]
-    values = [left.reshape(8 * n, 128), right.reshape(8 * n, 128)]
-    parts = [v.astype(BF16) for v in values]
-    if exact:
-        parts += [(v - p.astype(F32)).astype(BF16) for v, p in zip(values, parts)]
-    table = w_ref[dimension, : 128 * len(parts)]
-    total = jnp.dot(jnp.concatenate(parts, axis=1), table, preferred_element_type=F32)
-    return (total[:, :128] + total[:, 128:]).reshape(n, 8, 128)
+def merge(pairs, w_ref, dimension):
+    sides = [jnp.concatenate([pair[i] for pair in pairs], axis=0) for i in range(2)]
+    parts = [v.astype(BF16) for v in sides]
+    parts += [(v - p.astype(F32)).astype(BF16) for v, p in zip(sides, parts)]
+    total = jnp.dot(jnp.concatenate(parts, axis=1), w_ref[dimension], preferred_element_type=F32)
+    total = total[:, :128] + total[:, 128:]
+    return [total[8 * i : 8 * i + 8] for i in range(len(pairs))]
+
+
+def chunk_tiles(level, chunk):
+    if level < 3 or level > 4:
+        return [8 * chunk + i for i in range(8)]
+    lows = (2 * chunk, 2 * chunk + 1)
+    return [8 * high + low for high in range(4) for low in lows]
+
+
+def run_chunk(level, tiles, cos_ref, sin_ref, w_ref, state, sub):
+    e = (level + 1) % 2
+    turned = {}
+    for i in tiles:
+        re, im = state[0, i], state[1, i]
+        for j in range(2):
+            c, s = cos_ref[2 * level + j, i], sin_ref[2 * level + j, i]
+            turned[i, j] = (re * c - im * s, im * c + re * s)
+    pairs, places = [], []
+    for i in tiles:
+        for part in range(2):
+            if level < 5:
+                j = (i >> level) & 1
+                left = turned[i & ~(1 << level), j][part]
+                right = turned[i | 1 << level, j][part]
+            else:
+                left, right = turned[i, 0][part], turned[i, 1][part]
+                if level < 7:
+                    keep = ((sub >> (level - 4)) & 1) == 0
+                    shift = 1 << (level - 4)
+                    left, right = (
+                        jnp.where(keep, left, pltpu.roll(right, shift, 0)),
+                        jnp.where(keep, pltpu.roll(left, 8 - shift, 0), right),
+                    )
+            pairs.append((left, right))
+            places.append((part, i))
+    for (part, i), value in zip(places, merge(pairs, w_ref, e)):
+        state[part, i] = value
 
 
 def load(recv, state, lane):
@@ -224,43 +259,16 @@
 
 
 def run_levels(out_ref, cos_ref, sin_ref, w_ref, state, sub, lane):
+    for level in range(LEVELS):
+        for chunk in range(4):
+            run_chunk(level, chunk_tiles(level, chunk), cos_ref, sin_ref, w_ref, state, sub)
     low_lane = lane < 64
-    for level in range(LEVELS):
-        e = (level + 1) % 2
-        exact = level in EXACT
-        re, im = state[0], state[1]
-        turned = []
-        for j in range(2):
-            c, s = cos_ref[2 * level + j], sin_ref[2 * level + j]
-            turned.append((re * c - im * s, im * c + re * s))
-        for part in range(2):
-            r0, r1 = turned[0][part], turned[1][part]
-            if level < 5:
-                lo = 1 << level
-                hi = TILES // (2 * lo)
-                outs = []
-                for r in (r0, r1):
-                    v = r.reshape(hi, 2, lo, 8, 128)
-                    left = v[:, 0].reshape(16, 8, 128)
-                    right = v[:, 1].reshape(16, 8, 128)
-                    outs.append(merge(left, right, w_ref, e, exact).reshape(hi, 1, lo, 8, 128))
-                new = jnp.concatenate(outs, axis=1).reshape(TILES, 8, 128)
-            elif level < 7:
-                bit = level - 4
-                keep = (((sub >> bit) & 1) == 0)[None]
-                shift = 1 << bit
-                left = jnp.where(keep, r0, pltpu.roll(r1, shift, 1))
-                right = jnp.where(keep, pltpu.roll(r0, 8 - shift, 1), r1)
-                new = merge(left, right, w_ref, e, exact)
-            else:
-                new = merge(r0, r1, w_ref, e, exact)
-            state[part] = new
-    re, im = state[0], state[1]
-    c, s = cos_ref[2 * LEVELS], sin_ref[2 * LEVELS]
-    w_re, w_im = re * c + im * s, im * c - re * s
-    even = jnp.where(low_lane[None], w_re, pltpu.roll(w_im, 64, 2))
-    odd = jnp.where(low_lane[None], pltpu.roll(w_re, 64, 2), w_im)
-    out_ref[...] = jnp.concatenate([even[:, None], odd[:, None]], axis=1)
+    for i in range(TILES):
+        re, im = state[0, i], state[1, i]
+        c, s = cos_ref[2 * LEVELS, i], sin_ref[2 * LEVELS, i]
+        w_re, w_im = re * c + im * s, im * c - re * s
+        out_ref[i, 0] = jnp.where(low_lane, w_re, pltpu.roll(w_im, 64, 1))
+        out_ref[i, 1] = jnp.where(low_lane, pltpu.roll(w_re, 64, 1), w_im)
 
 
 FAR = 0xD0

time: 24 us -> 23.5 us (0.979)
  Pallas kernels: 23.2 us -> 22.7 us
    pallas_call x1, Pallas kernels: 23.2 us -> 22.7 us  [body(): pl.pallas_call(kernel, out_shape=pltpu.VMEM((TILES, 2, 8, 128), F32), in_...]
where the time goes in v4:
time: 23.5 us; the launch traced here: 23.4 us
  Pallas kernels  22.7 us (97%)
  local copies, waits for them, and re-layouts  0.71 us (3%)
    pallas_call x1, Pallas kernels, body(): pl.pallas_call(kernel, out_shape=pltpu.VMEM((TILES, 2, 8, 128), F32), in_...  22.7 us
    unnamed x1, local copies, waits for them, and re-layouts  0.71 us

profile of v4, /device:TPU:2, one launch (start us, length us, event | category | flops | bytes accessed | tf_op | source)
XLA Modules:
  0.0 23.4 jit_solution(4109157463844033568)
XLA Ops:
  0.0 22.7 %shard_map.46 = f32[32,2,8,128]{3,2,1,0:T(8,128)S(1)} custom-call(f32[256,2,128]{2,1,0:T(2,128)} %bitcast.3, f32[8,128]{1,0:T(8,128)} %constant.10.clone.tau_hbm, bf16[2,512,256]{2,1,0:T(8,128)(2,1)} %constant.31.w_hbm), custom_call_target="tpu_custom_call" | custom-call | tf_op jit(solution)/shard_map/pallas_call | solution.py:378
  22.7 0.7 %copy.6 = f32[512,128]{1,0:T(8,128)} copy(f32[512,128]{1,0:T(8,128)S(1)} %bitcast.2) | data formatting | bytes 524288

commit v5 on v4

--- a/solution.py
+++ b/solution.py
@@ -14,7 +14,7 @@
 GRID_N = 16384.0
 LEVELS = 8
 TILES = 32
-EARLY_PLANES = 2
+EARLY_PLANES = 3
 EXACT = (0, 1, 2, 3, 4, 5, 6, 7)
 
 
@@ -274,9 +274,11 @@
 FAR = 0xD0
 
 
-def kernel(x_ref, tau_hbm, w_hbm, out_ref, recv, state, g_ref, cos_ref, sin_ref, tau_ref, w_ref, send_sem, recv_sem, own_sem, table_sem, ready_sem):
+def kernel(x_ref, tau_hbm, w_hbm, out_ref, recv, state, g_ref, cos_ref, sin_ref, tau_ref, w_ref, held, send_sem, recv_sem, own_sem, table_sem, ready_sem, held_sem):
     me = lax.axis_index("outer") * 32 + lax.axis_index("inner")
     barrier = pltpu.get_barrier_semaphore()
+    hold = pltpu.make_async_copy(x_ref, held, held_sem)
+    hold.start()
 
     def greet(n, carry):
         pl.semaphore_signal(barrier, inc=1, device_id=me ^ (2 * n ^ FAR), device_id_type=LOGICAL)
@@ -307,12 +309,13 @@
     def _():
         factors()
 
+    hold.wait()
     pl.semaphore_wait(barrier, 128)
     pl.semaphore_signal(ready_sem, inc=1, device_id=me ^ 1, device_id_type=LOGICAL)
 
     def send(d):
         pltpu.make_async_remote_copy(
-            src_ref=x_ref.at[(d & 31) * 8 + (d >> 5)],
+            src_ref=held.at[(d & 31) * 8 + (d >> 5)],
             dst_ref=place,
             send_sem=send_sem,
             recv_sem=recv_sem,
@@ -388,11 +391,13 @@
             pltpu.VMEM((2 * LEVELS + 1, TILES, 8, 128), F32),
             pltpu.VMEM((8, 128), F32),
             pltpu.VMEM((2, 512, 256), BF16),
+            pltpu.VMEM((256, 2, 128), F32),
             pltpu.SemaphoreType.DMA,
             pltpu.SemaphoreType.DMA,
             pltpu.SemaphoreType.DMA,
             pltpu.SemaphoreType.DMA((2,)),
             pltpu.SemaphoreType.REGULAR,
+            pltpu.SemaphoreType.DMA,
         ],
         compiler_params=pltpu.CompilerParams(collective_id=0, has_side_effects=True),
     )(weights.reshape(256, 2, 128), jnp.asarray(tau, F32), jnp.stack(tables))

time: 23.5 us -> 23.3 us (level)
  no operation moved by 1% of the time
where the time goes in v5:
time: 23.3 us; the launch traced here: 23.2 us
  Pallas kernels  22.5 us (97%)
  local copies, waits for them, and re-layouts  0.71 us (3%)
    pallas_call x1, Pallas kernels, body(): pl.pallas_call(kernel, out_shape=pltpu.VMEM((TILES, 2, 8, 128), F32), in_...  22.5 us
    unnamed x1, local copies, waits for them, and re-layouts  0.71 us

profile of v5, /device:TPU:2, one launch (start us, length us, event | category | flops | bytes accessed | tf_op | source)
XLA Modules:
  0.0 23.2 jit_solution(14287892645712857492)
XLA Ops:
  0.0 22.5 %shard_map.46 = f32[32,2,8,128]{3,2,1,0:T(8,128)S(1)} custom-call(f32[256,2,128]{2,1,0:T(2,128)} %bitcast.3, f32[8,128]{1,0:T(8,128)} %constant.10.clone.tau_hbm, bf16[2,512,256]{2,1,0:T(8,128)(2,1)} %constant.31.w_hbm), custom_call_target="tpu_custom_call" | custom-call | tf_op jit(solution)/shard_map/pallas_call | solution.py:381
  22.5 0.7 %copy.6 = f32[512,128]{1,0:T(8,128)} copy(f32[512,128]{1,0:T(8,128)S(1)} %bitcast.2) | data formatting | bytes 524288

commit v6 on v5

--- a/solution.py
+++ b/solution.py
@@ -323,34 +323,36 @@
             device_id_type=LOGICAL,
         ).start()
 
-    def serve(other):
-        base = me ^ FAR ^ other
+    def serve(core, half):
+        base = ((me ^ FAR) & ~17) | core | 16 * half
 
         def step(n, carry):
-            send(base ^ (2 * n))
+            for m in range(8):
+                send(base ^ (32 * n) ^ (2 * m))
             return carry
 
-        lax.fori_loop(0, FAR // 2, step, 0, unroll=8)
-
-        @pl.when(other == 1)
+        lax.fori_loop(0, FAR >> 5, step, 0)
+
+        @pl.when((base ^ (FAR & 0xE0)) != me)
         def _():
-            send(base ^ FAR)
-
-        lax.fori_loop(FAR // 2 + 1, 128, step, 0, unroll=23)
-
-    core = me & 1
-
-    @pl.when(core == 0)
+            send(base ^ (FAR & 0xE0))
+
+        for m in range(1, 8):
+            send(base ^ (FAR & 0xE0) ^ (2 * m))
+        lax.fori_loop((FAR >> 5) + 1, 8, step, 0)
+
+    @pl.when(me & 1 == 0)
     def _():
         pl.semaphore_wait(ready_sem, 1)
 
-    serve(1 - core)
-
-    @pl.when(core == 1)
+    serve(1, 0)
+    @pl.when(me & 1 == 1)
     def _():
         pl.semaphore_wait(ready_sem, 1)
 
-    serve(core)
+    serve(0, 0)
+    serve(1, 1)
+    serve(0, 1)
     for copy in copies[1:]:
         copy.wait()
 

time: 23.3 us -> 22.6 us (0.970)
  Pallas kernels: 22.5 us -> 21.6 us
    pallas_call x1, Pallas kernels: 22.5 us -> 21.6 us  [body(): pl.pallas_call(kernel, out_shape=pltpu.VMEM((TILES, 2, 8, 128), F32), in_...]
where the time goes in v6:
time: 22.6 us; the launch traced here: 22.3 us
  Pallas kernels  21.6 us (96%)
  local copies, waits for them, and re-layouts  0.71 us (3%)
    pallas_call x1, Pallas kernels, body(): pl.pallas_call(kernel, out_shape=pltpu.VMEM((TILES, 2, 8, 128), F32), in_...  21.6 us
    unnamed x1, local copies, waits for them, and re-layouts  0.71 us

profile of v6, /device:TPU:2, one launch (start us, length us, event | category | flops | bytes accessed | tf_op | source)
XLA Modules:
  0.0 22.3 jit_solution(5861722302729599782)
XLA Ops:
  0.0 21.6 %shard_map.46 = f32[32,2,8,128]{3,2,1,0:T(8,128)S(1)} custom-call(f32[256,2,128]{2,1,0:T(2,128)} %bitcast.3, f32[8,128]{1,0:T(8,128)} %constant.10.clone.tau_hbm, bf16[2,512,256]{2,1,0:T(8,128)(2,1)} %constant.31.w_hbm), custom_call_target="tpu_custom_call" | custom-call | tf_op jit(solution)/shard_map/pallas_call | solution.py:383
  21.6 0.7 %copy.6 = f32[512,128]{1,0:T(8,128)} copy(f32[512,128]{1,0:T(8,128)S(1)} %bitcast.2) | data formatting | bytes 524288

commit v7 on v6

--- a/solution.py
+++ b/solution.py
@@ -331,7 +331,7 @@
                 send(base ^ (32 * n) ^ (2 * m))
             return carry
 
-        lax.fori_loop(0, FAR >> 5, step, 0)
+        lax.fori_loop(0, FAR >> 5, step, 0, unroll=True)
 
         @pl.when((base ^ (FAR & 0xE0)) != me)
         def _():
@@ -339,7 +339,7 @@
 
         for m in range(1, 8):
             send(base ^ (FAR & 0xE0) ^ (2 * m))
-        lax.fori_loop((FAR >> 5) + 1, 8, step, 0)
+        lax.fori_loop((FAR >> 5) + 1, 8, step, 0, unroll=True)
 
     @pl.when(me & 1 == 0)
     def _():

time: 22.6 us -> 22.6 us (level)
  no operation moved by 1% of the time
where the time goes in v7:
time: 22.6 us; the launch traced here: 22.4 us
  Pallas kernels  21.6 us (96%)
  local copies, waits for them, and re-layouts  0.71 us (3%)
    pallas_call x1, Pallas kernels, body(): pl.pallas_call(kernel, out_shape=pltpu.VMEM((TILES, 2, 8, 128), F32), in_...  21.6 us
    unnamed x1, local copies, waits for them, and re-layouts  0.71 us

profile of v7, /device:TPU:2, one launch (start us, length us, event | category | flops | bytes accessed | tf_op | source)
XLA Modules:
  0.0 22.4 jit_solution(2592333806091645124)
XLA Ops:
  0.0 21.6 %shard_map.46 = f32[32,2,8,128]{3,2,1,0:T(8,128)S(1)} custom-call(f32[256,2,128]{2,1,0:T(2,128)} %bitcast.3, f32[8,128]{1,0:T(8,128)} %constant.10.clone.tau_hbm, bf16[2,512,256]{2,1,0:T(8,128)(2,1)} %constant.31.w_hbm), custom_call_target="tpu_custom_call" | custom-call | tf_op jit(solution)/shard_map/pallas_call | solution.py:383
  21.7 0.7 %copy.6 = f32[512,128]{1,0:T(8,128)} copy(f32[512,128]{1,0:T(8,128)S(1)} %bitcast.2) | data formatting | bytes 524288

commit v8 on v7

--- a/solution.py
+++ b/solution.py
@@ -284,7 +284,7 @@
         pl.semaphore_signal(barrier, inc=1, device_id=me ^ (2 * n ^ FAR), device_id_type=LOGICAL)
         return carry
 
-    lax.fori_loop(0, FAR // 2, greet, 0, unroll=8)
+    lax.fori_loop(0, FAR // 2, greet, 0, unroll=True)
     lax.fori_loop(FAR // 2 + 1, 128, greet, 0, unroll=23)
     pl.semaphore_signal(barrier, inc=1, device_id=me ^ 1, device_id_type=LOGICAL)
     place = recv.at[me & 1, (me >> 1) & 31, me >> 6]

time: 22.6 us -> 22.4 us (level)
  no operation moved by 1% of the time
where the time goes in v8:
time: 22.4 us; the launch traced here: 22.2 us
  Pallas kernels  21.5 us (96%)
  local copies, waits for them, and re-layouts  0.71 us (3%)
    pallas_call x1, Pallas kernels, body(): pl.pallas_call(kernel, out_shape=pltpu.VMEM((TILES, 2, 8, 128), F32), in_...  21.5 us
    unnamed x1, local copies, waits for them, and re-layouts  0.71 us

profile of v8, /device:TPU:2, one launch (start us, length us, event | category | flops | bytes accessed | tf_op | source)
XLA Modules:
  0.0 22.2 jit_solution(696267870715995984)
XLA Ops:
  0.0 21.5 %shard_map.46 = f32[32,2,8,128]{3,2,1,0:T(8,128)S(1)} custom-call(f32[256,2,128]{2,1,0:T(2,128)} %bitcast.3, f32[8,128]{1,0:T(8,128)} %constant.10.clone.tau_hbm, bf16[2,512,256]{2,1,0:T(8,128)(2,1)} %constant.31.w_hbm), custom_call_target="tpu_custom_call" | custom-call | tf_op jit(solution)/shard_map/pallas_call | solution.py:383
  21.5 0.7 %copy.6 = f32[512,128]{1,0:T(8,128)} copy(f32[512,128]{1,0:T(8,128)S(1)} %bitcast.2) | data formatting | bytes 524288
